TPU v7x, 512 devices: a whole 4x8x8 slice. The times are simulated.
512 devices in a mesh: ctx: 128 (over y, z, x_hi), tp: 4 (over x_lo, core).
Axes of the slice: x: 4 (x_hi: 2, x_lo: 2; x = x_hi * 2 + x_lo), y: 8, z: 8, core: 2. Of those that a mesh axis runs over, the one named last changes fastest.
Arguments:
- q_input: bfloat16 [16384, 4096], P('ctx', 'tp'), may hold values from -6 to 6
- k_input: bfloat16 [16384, 4096], P('ctx', 'tp'), may hold values from -6 to 6
- v_input: bfloat16 [16384, 4096], P('ctx', 'tp'), may hold values from -6 to 6
- resid: bfloat16 [16384, 4096], P('ctx', 'tp'), may hold values from -18 to 18
- lengths: int32 [8], replicated, may hold values from 1 to 8192, 16384 in all
- short_filter: bfloat16 [3, 256, 7], P(None, 'tp'), may hold values from -2 to 2
- long_filter: bfloat16 [256, 128], P('tp'), may hold values from -0.5 to 0.5
- skip: float32 [4096], P('tp'), may hold values from -1 to 1
- gain: float32 [4096], P('tp'), may hold values from 0.1 to 1.9
- cotangent: bfloat16 [16384, 4096], P('ctx', 'tp'), may hold values from -12 to 12
Outputs:
- normed: bfloat16 [16384, 4096], P('ctx', 'tp')
- grad_q: bfloat16 [16384, 4096], P('ctx', 'tp')
- grad_k: bfloat16 [16384, 4096], P('ctx', 'tp')
- grad_v: bfloat16 [16384, 4096], P('ctx', 'tp')
- grad_short: float32 [3, 256, 7], P(None, 'tp')
- grad_long: float32 [256, 128], P('tp')
- grad_skip: float32 [4096], P('tp')
- grad_gain: float32 [4096], P('tp')
All inputs are finite; a program needn't handle non-finite values.
Results may differ from a plain program's by a relative error of at most 0.0047.
The roundings to bfloat16 on the way count: a program that leaves them out, or rounds other values in their place, can miss the bound.
Values may be sent and summed in bfloat16 or wider, within the bound.
A program may use at most 128 MiB of HBM per device.

v0:
```python
import functools

import jax
import jax.numpy as jnp
from jax import lax
from jax.experimental import pallas as pl
from jax.experimental.pallas import tpu as pltpu
from jax.sharding import PartitionSpec as P

C = 4096
GS = 16
K = 128
KS = 7
EPS = 1e-06
INNER = 16
MESH_ID = pl.DeviceIdType.MESH
F32 = jnp.float32
BF16 = jnp.bfloat16
HIGH = lax.Precision.HIGHEST
RIM = 8
HEAD = 16


def iota(shape, axis):
    return lax.broadcasted_iota(jnp.int32, shape, axis)


def skewed(x):
    return pltpu.roll(x, 0, 1, stride=1, stride_axis=0)


def body(
    count,
    tp_count,
    lengths,
    q_ref,
    k_ref,
    v_ref,
    resid_ref,
    cot_ref,
    short_ref,
    long_ref,
    skip_ref,
    gain_ref,
    normed_out,
    gq_out,
    gk_out,
    gv_out,
    gshort_out,
    glong_out,
    gskip_out,
    ggain_out,
    tail_s,
    tail_r,
    tail2_r,
    headk_r,
    headv_r,
    head_s,
    head_r,
    gext,
    gmx,
    gqs_s,
    gqs_r,
    xq,
    xk,
    xv,
    pk,
    pv,
    sq,
    sk,
    sv,
    mixed_s,
    summed_s,
    eq,
    ek,
    ev,
    fmat,
    umat,
    xmat,
    mats,
    xmasks,
    taps_m,
    prev_m,
    taps_w,
    wfwd,
    wrev,
    glong_s,
    tsum,
    stats,
    xs,
    first,
    second,
    result,
    hs,
    hr,
    ts,
    tr,
    s1,
    r1,
    s2,
    r2,
    s3,
    r3,
):
    length, width = q_ref.shape
    tiles = width // 128
    per = 128 // GS
    groups = width // GS
    ctx = lax.axis_index("ctx")
    tp = lax.axis_index("tp")
    outer = count // INNER
    hi = ctx // INNER
    lo = ctx % INNER
    total = count * length
    base = ctx * length

    def along(by):
        return (ctx + by + count) % count

    def inner_peer(k):
        return (lo + k) % INNER

    def outer_peer(k):
        return (hi + k) % outer

    def tp_peer(k):
        return (tp + k) % tp_count

    barrier = pltpu.get_barrier_semaphore()
    for by in (1, 2, -1, -2):
        pl.semaphore_signal(barrier, inc=1, device_id={"ctx": along(by)}, device_id_type=MESH_ID)
    for k in range(1, tp_count):
        pl.semaphore_signal(barrier, inc=1, device_id={"tp": tp_peer(k)}, device_id_type=MESH_ID)
    for k in range(1, INNER):
        pl.semaphore_signal(
            barrier, inc=1, device_id={"ctx": hi * INNER + inner_peer(k)}, device_id_type=MESH_ID
        )
    for k in range(1, outer):
        pl.semaphore_signal(
            barrier, inc=1, device_id={"ctx": outer_peer(k) * INNER + lo}, device_id_type=MESH_ID
        )

    def halo(slot, src, dst, by):
        return pltpu.make_async_remote_copy(
            src_ref=src,
            dst_ref=dst,
            send_sem=hs.at[slot],
            recv_sem=hr.at[slot],
            device_id={"ctx": along(by)},
            device_id_type=MESH_ID,
        )

    tails = halo(0, tail_s, tail_r, 1)
    tails2 = halo(1, tail_s.at[pl.ds(1, 2)], tail2_r, 2)
    heads_k = halo(2, k_ref.at[pl.ds(0, HEAD)], headk_r, 1)
    heads_v = halo(3, v_ref.at[pl.ds(0, HEAD)], headv_r, 1)
    heads_back = halo(4, head_s, head_r, -1)
    gated_copy = halo(5, gext.at[pl.ds(K + HEAD, K - HEAD)], gext.at[pl.ds(HEAD, K - HEAD)], 1)
    gm_copy = halo(6, gmx.at[pl.ds(0, K)], gmx.at[pl.ds(K, K)], -1)
    gm_far = halo(7, gmx.at[pl.ds(0, HEAD)], gmx.at[pl.ds(2 * K, HEAD)], -2)
    gqs_copy = halo(8, gqs_s, gqs_r, -1)

    for s, ref in enumerate((q_ref, k_ref, v_ref)):
        tail_s[s] = ref[length - HEAD :, :].astype(F32)[HEAD - RIM :].astype(BF16)
    head_s[0] = k_ref[0:HEAD, :].astype(F32)[:RIM].astype(BF16)
    head_s[1] = v_ref[0:HEAD, :].astype(F32)[:RIM].astype(BF16)

    pl.semaphore_wait(barrier, 4 + tp_count - 1 + INNER - 1 + outer - 1)
    tails.start()
    tails2.start()
    heads_k.start()
    heads_v.start()
    heads_back.start()

    starts = []
    at = jnp.int32(0)
    for i in range(lengths.shape[0]):
        starts.append(at)
        at = at + lengths[i]

    def position(token):
        begin = jnp.zeros_like(token)
        for start in starts:
            begin = jnp.where(token >= start, start, begin)
        return token - begin

    def flag(cond):
        return jnp.where(cond, 1.0, 0.0).astype(F32)

    token = base - RIM + iota((length + 2 * RIM, 128), 0)
    pos = position(token)
    for j in range(KS):
        taps_m[j] = flag((pos >= j) & (token < total))
    token = base - K + iota((HEAD, 128), 0)
    pos = position(token)
    for j in range(KS):
        prev_m[j] = flag(pos >= j)
    row = iota((K, 128), 0)
    col = iota((K, 128), 1)
    pos = position(base + row)
    mats[0] = flag((col > row) & (pos >= row - col + K))
    mats[1] = flag((col <= row) & (pos >= row - col))

    picks = flag(iota((groups, width), 1) // GS == iota((groups, width), 0)).astype(BF16)
    for s in range(3):
        table = lax.dot_general(
            short_ref[s], picks, (((0,), (0,)), ((), ())), preferred_element_type=F32
        )
        for t in range(tiles):
            taps_w[t, pl.ds(s * 8, KS), :] = table[:, t * 128 : (t + 1) * 128]

    def lanes(t):
        return pl.ds(pl.multiple_of(t * 128, 128), 128)

    def short_sum(buf, t, s, first_row, rows, mask, mask_row):
        result_sum = taps_w[t, pl.ds(s * 8, 1), :] * buf[t, pl.ds(RIM + first_row, rows), :]
        for j in range(1, KS):
            moved = buf[t, pl.ds(RIM + first_row - j, rows), :]
            result_sum = result_sum + taps_w[t, pl.ds(s * 8 + j, 1), :] * (
                moved * mask[j, pl.ds(mask_row, rows), :]
            )
        return result_sum

    rest = length - HEAD

    def gate_main(t, carry):
        xk[t, pl.ds(RIM, length), :] = k_ref[:, lanes(t)].astype(F32)
        xv[t, pl.ds(RIM, length), :] = v_ref[:, lanes(t)].astype(F32)
        ks = short_sum(xk, t, 1, HEAD, rest, taps_m, RIM + HEAD)
        vs = short_sum(xv, t, 2, HEAD, rest, taps_m, RIM + HEAD)
        sk[t, pl.ds(HEAD, rest), :] = ks
        sv[t, pl.ds(HEAD, rest), :] = vs
        gext[pl.ds(K + HEAD, rest), lanes(t)] = (ks * vs).astype(BF16)
        return carry

    lax.fori_loop(0, tiles, gate_main, 0)
    gated_copy.start()

    def query_main(t, carry):
        xq[t, pl.ds(RIM, length), :] = q_ref[:, lanes(t)].astype(F32)
        sq[t, pl.ds(HEAD, rest), :] = short_sum(xq, t, 0, HEAD, rest, taps_m, RIM + HEAD)
        return carry

    lax.fori_loop(0, tiles, query_main, 0)

    pos = position(base + col)
    mats[2] = flag((col >= row) & (pos >= col - row))
    token = base + K + col
    pos = position(token)
    mats[3] = flag((col < row) & (pos >= K + col - row) & (token < total))
    near_row = iota((8, 128), 0)
    near_col = iota((8, 128), 1)
    token = base + K + near_col
    pos = position(token)
    xmasks[0] = flag((near_col >= near_row) & (pos >= near_col - near_row) & (token < total))
    token = token + K
    pos = position(token)
    xmasks[1] = flag((near_col < near_row) & (pos >= K + near_col - near_row) & (token < total))

    flip = flag((row + col) % K == 0)
    wfwd[...] = long_ref[...].astype(F32)
    wrev[...] = jnp.dot(long_ref[...], flip.astype(BF16), preferred_element_type=F32)

    def build(t, carry):
        forward = wfwd[pl.ds(pl.multiple_of(t * per, per), per), :]
        backward = wrev[pl.ds(pl.multiple_of(t * per, per), per), :]
        extra = []
        for g in range(per):
            band = skewed(jnp.broadcast_to(backward[g : g + 1, :], (K, K)))
            fmat[t, pl.ds(g * K, K), pl.ds(0, K)] = (band * mats[0]).astype(BF16)
            fmat[t, pl.ds(g * K, K), pl.ds(K, K)] = (band * mats[1]).astype(BF16)
            band = skewed(jnp.broadcast_to(forward[g : g + 1, :], (K, K)))
            umat[t, pl.ds(g * K, K), pl.ds(0, K)] = (band * mats[2]).astype(BF16)
            umat[t, pl.ds(g * K, K), pl.ds(K, K)] = (band * mats[3]).astype(BF16)
            near = band[0:8, :]
            extra.append(jnp.concatenate([near * xmasks[0], near * xmasks[1]], axis=1))
        xmat[t] = jnp.concatenate(extra, axis=0).astype(BF16)
        return carry

    lax.fori_loop(0, tiles, build, 0)
    gmx[pl.ds(2 * K + HEAD, K - HEAD), :] = jnp.zeros((K - HEAD, width), BF16)

    tails.wait_recv()
    tails2.wait_recv()
    heads_k.wait_recv()
    heads_v.wait_recv()
    heads_back.wait_recv()
    for t in range(tiles):
        part = slice(t * 128, (t + 1) * 128)
        for s, buf in enumerate((xq, xk, xv)):
            buf[t, pl.ds(0, RIM), :] = tail_r[s, :, part].astype(F32)
        for s, (buf, prev, head) in enumerate(((xk, pk, headk_r), (xv, pv, headv_r))):
            buf[t, pl.ds(RIM + length, RIM), :] = head_r[s, :, part].astype(F32)
            prev[t, pl.ds(0, RIM), :] = tail2_r[s, :, part].astype(F32)
            prev[t, pl.ds(RIM, HEAD), :] = head[:, part].astype(F32)

    def gate_rims(t, carry):
        sq[t, pl.ds(0, HEAD), :] = short_sum(xq, t, 0, 0, HEAD, taps_m, RIM)
        ks = short_sum(xk, t, 1, 0, HEAD, taps_m, RIM)
        vs = short_sum(xv, t, 2, 0, HEAD, taps_m, RIM)
        sk[t, pl.ds(0, HEAD), :] = ks
        sv[t, pl.ds(0, HEAD), :] = vs
        gext[pl.ds(K, HEAD), lanes(t)] = (ks * vs).astype(BF16)
        sk[t, pl.ds(length, RIM), :] = short_sum(xk, t, 1, length, RIM, taps_m, RIM + length)
        sv[t, pl.ds(length, RIM), :] = short_sum(xv, t, 2, length, RIM, taps_m, RIM + length)
        ks = short_sum(pk, t, 1, 0, HEAD, prev_m, 0)
        vs = short_sum(pv, t, 2, 0, HEAD, prev_m, 0)
        gext[pl.ds(0, HEAD), lanes(t)] = (ks * vs).astype(BF16)
        return carry

    lax.fori_loop(0, tiles, gate_rims, 0)
    gated_copy.wait_recv()

    def select(products, rows):
        group = iota((rows, 128), 1) // GS
        picked = products[0:rows]
        for g in range(1, per):
            picked = jnp.where(group == g, products[g * rows : (g + 1) * rows], picked)
        return picked

    def mix(t, carry):
        squares, products = carry
        source = gext[:, lanes(t)]
        conv = select(jnp.dot(fmat[t], source, preferred_element_type=F32), K)
        gated = gext[pl.ds(K, K), lanes(t)].astype(F32)
        mixed = conv + skip_ref[:, lanes(t)] * gated
        summed = resid_ref[:, lanes(t)].astype(F32) + sq[t] * mixed
        mixed_s[t] = mixed
        summed_s[t] = summed
        squares = squares + summed * summed
        products = products + gain_ref[:, lanes(t)] * cot_ref[:, lanes(t)].astype(F32) * summed
        return squares, products

    zero = jnp.zeros((length, 128), F32)
    squares, products = lax.fori_loop(0, tiles, mix, (zero, zero))
    squares = jnp.sum(squares.T, axis=0, keepdims=True)
    products = jnp.sum(products.T, axis=0, keepdims=True)
    stats[tp] = jnp.where(near_row == 0, squares, products)

    def share(k):
        return pltpu.make_async_remote_copy(
            src_ref=stats.at[tp],
            dst_ref=stats.at[tp],
            send_sem=ts.at[k],
            recv_sem=tr.at[tp],
            device_id={"tp": tp_peer(k)},
            device_id_type=MESH_ID,
        )

    def arrived(sem, buf, slot):
        pltpu.make_async_copy(buf.at[slot], buf.at[slot], sem.at[slot]).wait()

    for k in range(1, tp_count):
        share(k).start()
    for k in range(1, tp_count):
        arrived(tr, stats, tp_peer(tp_count - k))
    both = stats[0]
    for i in range(1, tp_count):
        both = both + stats[i]
    both = both / (width * tp_count)
    shifted = both[0:1] + EPS
    inverse_row = lax.rsqrt(shifted)
    inverse_row = inverse_row * (1.5 - 0.5 * shifted * inverse_row * inverse_row)
    pull_row = inverse_row * inverse_row * both[1:2]
    inverse = jnp.broadcast_to(inverse_row, (128, length)).T
    pull = jnp.broadcast_to(pull_row, (128, length)).T
    mats[4] = inverse
    mats[5] = pull

    def grads(t, carry):
        inverse = mats[4]
        summed = summed_s[t]
        gain = gain_ref[:, lanes(t)]
        cot = cot_ref[:, lanes(t)].astype(F32)
        normed_out[:, lanes(t)] = (gain * summed * inverse).astype(BF16)
        grad_sum = inverse * (gain * cot - summed * mats[5])
        grad_mixed = (grad_sum * sq[t]).astype(BF16)
        gmx[pl.ds(0, K), lanes(t)] = grad_mixed
        grad_qs = (grad_sum * mixed_s[t]).astype(BF16)
        eq[t, pl.ds(0, length), :] = grad_qs.astype(F32)
        gqs_s[:, lanes(t)] = grad_qs.astype(F32)[:RIM].astype(BF16)
        gated = gext[pl.ds(K, K), lanes(t)].astype(F32)
        xs[8, pl.ds(t, 1), :] = jnp.sum(grad_mixed.astype(F32) * gated, axis=0, keepdims=True)
        xs[9, pl.ds(t, 1), :] = jnp.sum(cot * summed * inverse, axis=0, keepdims=True)
        return carry

    lax.fori_loop(0, tiles, grads, 0)
    gm_copy.start()
    gm_far.start()
    gqs_copy.start()

    def correlate(t, carry):
        grad_mixed = gmx[pl.ds(0, K), lanes(t)]
        source = gext[:, lanes(t)]
        group = iota((K, 128), 1) // GS
        left = jnp.concatenate(
            [jnp.where(group == g, grad_mixed, jnp.zeros_like(grad_mixed)) for g in range(per)], axis=0
        )
        cross = lax.dot_general(
            left, source, (((1,), (1,)), ((), ())), preferred_element_type=F32
        )
        for g in range(per):
            block = cross[g * K : (g + 1) * K]
            band = block[:, :K] * mats[0] + block[:, K:] * mats[1]
            folded = band[0:8]
            for a in range(1, K // 8):
                folded = folded + pltpu.roll(band[a * 8 : (a + 1) * 8], K - a * 8, 1)
            glong_s[pl.ds(pl.multiple_of(t * per * 8, 8) + g * 8, 8), :] = folded
        return carry

    lax.fori_loop(0, tiles, correlate, 0)
    folded = glong_s[pl.ds(0, groups, stride=8), :]
    for b in range(1, 8):
        folded = folded + pltpu.roll(glong_s[pl.ds(b, groups, stride=8), :], K - b, 1)
    turned = jnp.dot(folded, flip, precision=HIGH, preferred_element_type=F32)
    for t in range(tiles):
        xs[t] = turned[t * per : (t + 1) * per]
    tsum[...] = jnp.zeros_like(tsum)

    gm_copy.wait_recv()
    gm_far.wait_recv()
    gqs_copy.wait_recv()

    def back(t, carry):
        conv = select(
            jnp.dot(umat[t], gmx[pl.ds(0, 2 * K), lanes(t)], preferred_element_type=F32), K
        )
        extra = select(
            jnp.dot(xmat[t], gmx[pl.ds(K, 2 * K), lanes(t)], preferred_element_type=F32), 8
        )
        skip = skip_ref[:, lanes(t)]
        grad_gated = skip * gmx[pl.ds(0, K), lanes(t)].astype(F32) + conv
        ek[t, pl.ds(0, length), :] = (grad_gated * sv[t, pl.ds(0, length), :]).astype(BF16).astype(F32)
        ev[t, pl.ds(0, length), :] = (grad_gated * sk[t, pl.ds(0, length), :]).astype(BF16).astype(F32)
        near = gmx[pl.ds(K, HEAD), lanes(t)].astype(F32)[:RIM]
        grad_gated = skip * near + extra
        ek[t, pl.ds(length, RIM), :] = (grad_gated * sv[t, pl.ds(length, RIM), :]).astype(BF16).astype(F32)
        ev[t, pl.ds(length, RIM), :] = (grad_gated * sk[t, pl.ds(length, RIM), :]).astype(BF16).astype(F32)
        eq[t, pl.ds(length, RIM), :] = gqs_r[:, lanes(t)].astype(F32)
        for s, (buf, values, out) in enumerate(((eq, xq, gq_out), (ek, xk, gk_out), (ev, xv, gv_out))):
            own = values[t, pl.ds(RIM, length), :]
            result_sum = jnp.zeros((length, 128), F32)
            for j in range(KS):
                moved = buf[t, pl.ds(j, length), :] * taps_m[j, pl.ds(RIM + j, length), :]
                result_sum = result_sum + taps_w[t, pl.ds(s * 8 + j, 1), :] * moved
                tsum[t, pl.ds(s * 8 + j, 1), :] = jnp.sum(moved * own, axis=0, keepdims=True)
            out[:, lanes(t)] = result_sum.astype(BF16)
        return carry

    lax.fori_loop(0, tiles, back, 0)

    short_sums = jnp.zeros((24, 128), F32)
    for t in range(tiles):
        spread = flag(iota((128, 128), 0) // GS + t * per == iota((128, 128), 1))
        short_sums = short_sums + jnp.dot(
            tsum[t], spread, precision=HIGH, preferred_element_type=F32
        )
    for s in range(3):
        xs[10 + s] = short_sums[s * 8 : (s + 1) * 8]
    for i in range(13, INNER):
        xs[i] = jnp.zeros((8, 128), F32)

    def scatter(k):
        peer = inner_peer(k)
        return pltpu.make_async_remote_copy(
            src_ref=xs.at[peer],
            dst_ref=first.at[lo],
            send_sem=s1.at[k],
            recv_sem=r1.at[lo],
            device_id={"ctx": hi * INNER + peer},
            device_id_type=MESH_ID,
        )

    def exchange(k):
        return pltpu.make_async_remote_copy(
            src_ref=second.at[hi],
            dst_ref=second.at[hi],
            send_sem=s2.at[k],
            recv_sem=r2.at[hi],
            device_id={"ctx": outer_peer(k) * INNER + lo},
            device_id_type=MESH_ID,
        )

    def gather(k):
        return pltpu.make_async_remote_copy(
            src_ref=result.at[lo],
            dst_ref=result.at[lo],
            send_sem=s3.at[k],
            recv_sem=r3.at[lo],
            device_id={"ctx": hi * INNER + inner_peer(k)},
            device_id_type=MESH_ID,
        )

    for k in range(1, INNER):
        scatter(k).start()
    sums = xs[lo]
    for k in range(1, INNER):
        slot = inner_peer(INNER - k)
        arrived(r1, first, slot)
        sums = sums + first[slot]
    second[hi] = sums
    for k in range(1, outer):
        exchange(k).start()
    for k in range(1, outer):
        arrived(r2, second, outer_peer(outer - k))
    sums = second[0]
    for i in range(1, outer):
        sums = sums + second[i]
    result[lo] = sums
    for k in range(1, INNER):
        gather(k).start()

    for copy in (
        tails,
        tails2,
        heads_k,
        heads_v,
        heads_back,
        gated_copy,
        gm_copy,
        gm_far,
        gqs_copy,
    ):
        copy.wait_send()
    for k in range(1, tp_count):
        share(k).wait_send()
    for k in range(1, INNER):
        scatter(k).wait_send()
    for k in range(1, outer):
        exchange(k).wait_send()
    for k in range(1, INNER):
        arrived(r3, result, inner_peer(INNER - k))

    for t in range(tiles):
        glong_out[pl.ds(t * per, per), :] = result[t]
    gskip_out[...] = result[8]
    ggain_out[...] = result[9]
    for s in range(3):
        gshort_out[s] = result[10 + s].T[:groups, :KS]
    for k in range(1, INNER):
        gather(k).wait_send()


def shards(
    q_input, k_input, v_input, resid, lengths, short_filter, long_filter, skip, gain, cotangent
):
    length, width = q_input.shape
    tiles = width // 128
    groups = width // GS
    per = 128 // GS
    count = lax.axis_size("ctx")
    tp_count = lax.axis_size("tp")
    outer = count // INNER
    vmem = pl.BlockSpec(memory_space=pltpu.VMEM)
    large = jax.ShapeDtypeStruct((length, width), BF16)

    def tiled(rows):
        return pltpu.VMEM((tiles, rows, 128), F32)

    dma = pltpu.SemaphoreType.DMA
    outs = pl.pallas_call(
        functools.partial(body, count, tp_count),
        out_shape=(
            large,
            large,
            large,
            large,
            jax.ShapeDtypeStruct((3, groups, KS), F32),
            jax.ShapeDtypeStruct((groups, K), F32),
            jax.ShapeDtypeStruct((tiles, 128), F32),
            jax.ShapeDtypeStruct((tiles, 128), F32),
        ),
        in_specs=[pl.BlockSpec(memory_space=pltpu.SMEM)] + [vmem] * 9,
        out_specs=(vmem,) * 8,
        scratch_shapes=[
            pltpu.VMEM((3, RIM, width), BF16),
            pltpu.VMEM((3, RIM, width), BF16),
            pltpu.VMEM((2, RIM, width), BF16),
            pltpu.VMEM((HEAD, width), BF16),
            pltpu.VMEM((HEAD, width), BF16),
            pltpu.VMEM((2, RIM, width), BF16),
            pltpu.VMEM((2, RIM, width), BF16),
            pltpu.VMEM((2 * K, width), BF16),
            pltpu.VMEM((3 * K, width), BF16),
            pltpu.VMEM((RIM, width), BF16),
            pltpu.VMEM((RIM, width), BF16),
            tiled(length + 2 * RIM),
            tiled(length + 2 * RIM),
            tiled(length + 2 * RIM),
            tiled(RIM + HEAD),
            tiled(RIM + HEAD),
            tiled(length),
            tiled(length + RIM),
            tiled(length + RIM),
            tiled(length),
            tiled(length),
            tiled(length + RIM),
            tiled(length + RIM),
            tiled(length + RIM),
            pltpu.VMEM((tiles, per * K, 2 * K), BF16),
            pltpu.VMEM((tiles, per * K, 2 * K), BF16),
            pltpu.VMEM((tiles, per * 8, 2 * K), BF16),
            pltpu.VMEM((6, K, 128), F32),
            pltpu.VMEM((2, 8, 128), F32),
            pltpu.VMEM((KS, length + 2 * RIM, 128), F32),
            pltpu.VMEM((KS, HEAD, 128), F32),
            tiled(24),
            pltpu.VMEM((groups, K), F32),
            pltpu.VMEM((groups, K), F32),
            pltpu.VMEM((groups * 8, K), F32),
            tiled(24),
            pltpu.VMEM((tp_count, 8, 128), F32),
            pltpu.VMEM((INNER, 8, 128), F32),
            pltpu.VMEM((INNER, 8, 128), F32),
            pltpu.VMEM((outer, 8, 128), F32),
            pltpu.VMEM((INNER, 8, 128), F32),
            dma((9,)),
            dma((9,)),
            dma((tp_count,)),
            dma((tp_count,)),
            dma((INNER,)),
            dma((INNER,)),
            dma((outer,)),
            dma((outer,)),
            dma((INNER,)),
            dma((INNER,)),
        ],
        compiler_params=pltpu.CompilerParams(collective_id=0, has_side_effects=True),
        name="operator",
    )(
        lengths,
        q_input,
        k_input,
        v_input,
        resid,
        cotangent,
        short_filter,
        long_filter,
        skip.reshape(1, width),
        gain.reshape(1, width),
    )
    return outs[:6] + (outs[6].reshape(width), outs[7].reshape(width))


def solution(mesh):
    rows = P("ctx", "tp")
    return jax.shard_map(
        shards,
        mesh=mesh,
        in_specs=(
            rows,
            rows,
            rows,
            rows,
            P(),
            P(None, "tp", None),
            P("tp", None),
            P("tp"),
            P("tp"),
            rows,
        ),
        out_specs=(rows, rows, rows, rows, P(None, "tp", None), P("tp", None), P("tp"), P("tp")),
        check_vma=False,
    )
```

profile of v0, /device:TPU:6, one launch (start us, length us, event | category | flops | bytes accessed | tf_op | source)
XLA Modules:
  0.0 76.8 jit_solution(8426035703545752574)
XLA Ops:
  0.6 1.4 %copy.18.short_ref = bf16[3,64,7]{2,1,0:T(8,128)(2,1)} copy(bf16[3,64,7]{1,2,0:T(8,128)(2,1)} %param.15) | data formatting | bytes 5376 | tf_op args[5]
  2.1 66.6 %operator.1 = (bf16[128,1024]{1,0:T(8,128)(2,1)}, bf16[128,1024]{1,0:T(8,128)(2,1)}, bf16[128,1024]{1,0:T(8,128)(2,1)}, bf16[128,1024]{1,0:T(8,128)(2,1)}, f32[3...) custom-call(s32[8]{0:T(128)} %lengths.1, bf16[128,1024]{1,0:T(8,128)(2,1)} %q_ref.1, ...), custom_call_target="tpu_custom_call" | custom-call | tf_op jit(solution)/shard_map/operator/pallas_call | solution.py:561
  68.7 1.6 %copy.19 = f32[3,64,7]{1,2,0:T(8,128)} copy(f32[3,64,7]{2,1,0:T(8,128)} %get-tuple-element.28) | data formatting | bytes 10752
  70.2 0.0 copy-start.2
  70.2 1.7 %copy.27 = bf16[128,1024]{1,0:T(8,128)(2,1)} copy(bf16[128,1024]{1,0:T(8,128)(2,1)} %get-tuple-element.40) | data formatting | bytes 524288
  72.0 0.0 copy-done.2
  72.0 0.0 copy-start.1
  72.0 0.7 copy.28
  72.7 0.3 copy-done.1
  73.0 0.0 copy-start
  73.0 0.7 copy.29
  73.7 0.3 copy-done
  74.1 0.0 copy-start.3
  74.1 0.7 copy.30
  74.8 0.1 copy-done.3
  74.8 0.0 copy-start.5
  74.8 0.6 copy.31
  75.4 0.1 copy-done.5
  75.5 0.0 copy-start.4
  75.5 0.6 copy.32
  76.1 0.1 copy-done.4
  76.2 0.6 copy.33
Async XLA Ops:
  70.2 1.7 %copy-start.2 = (bf16[128,1024]{1,0:T(8,128)(2,1)S(1)}, bf16[128,1024]{1,0:T(8,128)(2,1)}, u32[]{:S(2)}) copy-start(bf16[128,1024]{1,0:T(8,128)(2,1)} %get-tuple-element.41) | copy-start | bytes 786436
  72.0 1.0 %copy-start.1 = (bf16[128,1024]{1,0:T(8,128)(2,1)S(1)}, bf16[128,1024]{1,0:T(8,128)(2,1)}, u32[]{:S(2)}) copy-start(bf16[128,1024]{1,0:T(8,128)(2,1)} %get-tuple-element.42) | copy-start | bytes 786436
  73.0 1.0 %copy-start = (bf16[128,1024]{1,0:T(8,128)(2,1)S(1)}, bf16[128,1024]{1,0:T(8,128)(2,1)}, u32[]{:S(2)}) copy-start(bf16[128,1024]{1,0:T(8,128)(2,1)} %get-tuple-element.43) | copy-start | bytes 786436
  74.1 0.8 copy-start.3
  74.8 0.7 copy-start.5
  75.5 0.7 copy-start.4
where the time goes:
time: 77.2 us; the launch traced here: 76.8 us
  Pallas kernels  66.6 us (86%)
  local copies, waits for them, and re-layouts  9.53 us (12%)
    pallas_call x1, Pallas kernels, shards(): pl.pallas_call(functools.partial(body, count, tp_count), out_shape=(large...  66.6 us
    unnamed x21, local copies, waits for them, and re-layouts  9.53 us

commit v1 on v0

--- a/solution.py
+++ b/solution.py
@@ -19,6 +19,7 @@
 HIGH = lax.Precision.HIGHEST
 RIM = 8
 HEAD = 16
+CHUNKS = 4
 
 
 def iota(shape, axis):
@@ -85,7 +86,6 @@
     wfwd,
     wrev,
     glong_s,
-    tsum,
     stats,
     xs,
     first,
@@ -101,6 +101,17 @@
     r2,
     s3,
     r3,
+    near_s,
+    far_s,
+    s4,
+    r4,
+    s5,
+    r5,
+    normed_b,
+    gq_b,
+    gk_b,
+    gv_b,
+    os,
 ):
     length, width = q_ref.shape
     tiles = width // 128
@@ -155,22 +166,29 @@
     heads_k = halo(2, k_ref.at[pl.ds(0, HEAD)], headk_r, 1)
     heads_v = halo(3, v_ref.at[pl.ds(0, HEAD)], headv_r, 1)
     heads_back = halo(4, head_s, head_r, -1)
-    gated_copy = halo(5, gext.at[pl.ds(K + HEAD, K - HEAD)], gext.at[pl.ds(HEAD, K - HEAD)], 1)
-    gm_copy = halo(6, gmx.at[pl.ds(0, K)], gmx.at[pl.ds(K, K)], -1)
-    gm_far = halo(7, gmx.at[pl.ds(0, HEAD)], gmx.at[pl.ds(2 * K, HEAD)], -2)
-    gqs_copy = halo(8, gqs_s, gqs_r, -1)
+    gm_far = halo(5, gmx.at[:, pl.ds(0, HEAD)], gmx.at[:, pl.ds(2 * K, HEAD)], -2)
+    gqs_copy = halo(6, gqs_s, gqs_r, -1)
+    each = tiles // CHUNKS
+    gated_copies = []
+    gm_copies = []
+    for c in range(CHUNKS):
+        some = pl.ds(c * each, each)
+        gated_copies.append(
+            halo(
+                7 + c,
+                gext.at[some, pl.ds(K + HEAD, K - HEAD)],
+                gext.at[some, pl.ds(HEAD, K - HEAD)],
+                1,
+            )
+        )
+        gm_copies.append(
+            halo(7 + CHUNKS + c, gmx.at[some, pl.ds(0, K)], gmx.at[some, pl.ds(K, K)], -1)
+        )
 
     for s, ref in enumerate((q_ref, k_ref, v_ref)):
         tail_s[s] = ref[length - HEAD :, :].astype(F32)[HEAD - RIM :].astype(BF16)
     head_s[0] = k_ref[0:HEAD, :].astype(F32)[:RIM].astype(BF16)
     head_s[1] = v_ref[0:HEAD, :].astype(F32)[:RIM].astype(BF16)
-
-    pl.semaphore_wait(barrier, 4 + tp_count - 1 + INNER - 1 + outer - 1)
-    tails.start()
-    tails2.start()
-    heads_k.start()
-    heads_v.start()
-    heads_back.start()
 
     starts = []
     at = jnp.int32(0)
@@ -203,9 +221,7 @@
 
     picks = flag(iota((groups, width), 1) // GS == iota((groups, width), 0)).astype(BF16)
     for s in range(3):
-        table = lax.dot_general(
-            short_ref[s], picks, (((0,), (0,)), ((), ())), preferred_element_type=F32
-        )
+        table = jnp.dot(short_ref[s], picks, preferred_element_type=F32)
         for t in range(tiles):
             taps_w[t, pl.ds(s * 8, KS), :] = table[:, t * 128 : (t + 1) * 128]
 
@@ -230,11 +246,18 @@
         vs = short_sum(xv, t, 2, HEAD, rest, taps_m, RIM + HEAD)
         sk[t, pl.ds(HEAD, rest), :] = ks
         sv[t, pl.ds(HEAD, rest), :] = vs
-        gext[pl.ds(K + HEAD, rest), lanes(t)] = (ks * vs).astype(BF16)
+        gext[t, pl.ds(K + HEAD, rest), :] = (ks * vs).astype(BF16)
         return carry
 
     lax.fori_loop(0, tiles, gate_main, 0)
-    gated_copy.start()
+    pl.semaphore_wait(barrier, 4 + tp_count - 1 + INNER - 1 + outer - 1)
+    tails.start()
+    tails2.start()
+    heads_k.start()
+    heads_v.start()
+    heads_back.start()
+    for copy in gated_copies:
+        copy.start()
 
     def query_main(t, carry):
         xq[t, pl.ds(RIM, length), :] = q_ref[:, lanes(t)].astype(F32)
@@ -278,7 +301,7 @@
         return carry
 
     lax.fori_loop(0, tiles, build, 0)
-    gmx[pl.ds(2 * K + HEAD, K - HEAD), :] = jnp.zeros((K - HEAD, width), BF16)
+    gmx[:, pl.ds(2 * K + HEAD, K - HEAD), :] = jnp.zeros((tiles, K - HEAD, 128), BF16)
 
     tails.wait_recv()
     tails2.wait_recv()
@@ -300,16 +323,15 @@
         vs = short_sum(xv, t, 2, 0, HEAD, taps_m, RIM)
         sk[t, pl.ds(0, HEAD), :] = ks
         sv[t, pl.ds(0, HEAD), :] = vs
-        gext[pl.ds(K, HEAD), lanes(t)] = (ks * vs).astype(BF16)
+        gext[t, pl.ds(K, HEAD), :] = (ks * vs).astype(BF16)
         sk[t, pl.ds(length, RIM), :] = short_sum(xk, t, 1, length, RIM, taps_m, RIM + length)
         sv[t, pl.ds(length, RIM), :] = short_sum(xv, t, 2, length, RIM, taps_m, RIM + length)
         ks = short_sum(pk, t, 1, 0, HEAD, prev_m, 0)
         vs = short_sum(pv, t, 2, 0, HEAD, prev_m, 0)
-        gext[pl.ds(0, HEAD), lanes(t)] = (ks * vs).astype(BF16)
+        gext[t, pl.ds(0, HEAD), :] = (ks * vs).astype(BF16)
         return carry
 
     lax.fori_loop(0, tiles, gate_rims, 0)
-    gated_copy.wait_recv()
 
     def select(products, rows):
         group = iota((rows, 128), 1) // GS
@@ -320,9 +342,9 @@
 
     def mix(t, carry):
         squares, products = carry
-        source = gext[:, lanes(t)]
+        source = gext[t]
         conv = select(jnp.dot(fmat[t], source, preferred_element_type=F32), K)
-        gated = gext[pl.ds(K, K), lanes(t)].astype(F32)
+        gated = gext[t, pl.ds(K, K), :].astype(F32)
         mixed = conv + skip_ref[:, lanes(t)] * gated
         summed = resid_ref[:, lanes(t)].astype(F32) + sq[t] * mixed
         mixed_s[t] = mixed
@@ -332,7 +354,10 @@
         return squares, products
 
     zero = jnp.zeros((length, 128), F32)
-    squares, products = lax.fori_loop(0, tiles, mix, (zero, zero))
+    squares, products = zero, zero
+    for c in range(CHUNKS):
+        gated_copies[c].wait_recv()
+        squares, products = lax.fori_loop(c * each, (c + 1) * each, mix, (squares, products))
     squares = jnp.sum(squares.T, axis=0, keepdims=True)
     products = jnp.sum(products.T, axis=0, keepdims=True)
     stats[tp] = jnp.where(near_row == 0, squares, products)
@@ -372,26 +397,34 @@
         summed = summed_s[t]
         gain = gain_ref[:, lanes(t)]
         cot = cot_ref[:, lanes(t)].astype(F32)
-        normed_out[:, lanes(t)] = (gain * summed * inverse).astype(BF16)
+        normed_b[:, lanes(t)] = (gain * summed * inverse).astype(BF16)
         grad_sum = inverse * (gain * cot - summed * mats[5])
         grad_mixed = (grad_sum * sq[t]).astype(BF16)
-        gmx[pl.ds(0, K), lanes(t)] = grad_mixed
+        gmx[t, pl.ds(0, K), :] = grad_mixed
         grad_qs = (grad_sum * mixed_s[t]).astype(BF16)
         eq[t, pl.ds(0, length), :] = grad_qs.astype(F32)
         gqs_s[:, lanes(t)] = grad_qs.astype(F32)[:RIM].astype(BF16)
-        gated = gext[pl.ds(K, K), lanes(t)].astype(F32)
+        gated = gext[t, pl.ds(K, K), :].astype(F32)
         xs[8, pl.ds(t, 1), :] = jnp.sum(grad_mixed.astype(F32) * gated, axis=0, keepdims=True)
         xs[9, pl.ds(t, 1), :] = jnp.sum(cot * summed * inverse, axis=0, keepdims=True)
         return carry
 
     lax.fori_loop(0, tiles, grads, 0)
-    gm_copy.start()
+    gqs_copy.start()
     gm_far.start()
-    gqs_copy.start()
+    for copy in gm_copies:
+        copy.start()
+    stores = [
+        pltpu.make_async_copy(buf, out, os.at[i])
+        for i, (buf, out) in enumerate(
+            ((normed_b, normed_out), (gq_b, gq_out), (gk_b, gk_out), (gv_b, gv_out))
+        )
+    ]
+    stores[0].start()
 
     def correlate(t, carry):
-        grad_mixed = gmx[pl.ds(0, K), lanes(t)]
-        source = gext[:, lanes(t)]
+        grad_mixed = gmx[t, pl.ds(0, K), :]
+        source = gext[t]
         group = iota((K, 128), 1) // GS
         left = jnp.concatenate(
             [jnp.where(group == g, grad_mixed, jnp.zeros_like(grad_mixed)) for g in range(per)], axis=0
@@ -415,92 +448,109 @@
     turned = jnp.dot(folded, flip, precision=HIGH, preferred_element_type=F32)
     for t in range(tiles):
         xs[t] = turned[t * per : (t + 1) * per]
-    tsum[...] = jnp.zeros_like(tsum)
-
-    gm_copy.wait_recv()
+    for i in range(10, INNER):
+        xs[i] = jnp.zeros((8, 128), F32)
+
+    def copy_to(src, dst, send, recv, device):
+        return pltpu.make_async_remote_copy(
+            src_ref=src,
+            dst_ref=dst,
+            send_sem=send,
+            recv_sem=recv,
+            device_id={"ctx": device},
+            device_id_type=MESH_ID,
+        )
+
+    def inner_device(k):
+        return hi * INNER + inner_peer(k)
+
+    def outer_device(k):
+        return outer_peer(k) * INNER + lo
+
+    def scatter(k):
+        return copy_to(xs.at[inner_peer(k)], first.at[lo], s1.at[k], r1.at[lo], inner_device(k))
+
+    def exchange(k):
+        return copy_to(second.at[hi], second.at[hi], s2.at[k], r2.at[hi], outer_device(k))
+
+    def gather(k):
+        return copy_to(result.at[lo], result.at[lo], s3.at[k], r3.at[lo], inner_device(k))
+
+    def near_sums(k):
+        return copy_to(near_s.at[lo], near_s.at[lo], s4.at[k], r4.at[lo], inner_device(k))
+
+    def far_sums(k):
+        return copy_to(far_s.at[hi], far_s.at[hi], s5.at[k], r5.at[hi], outer_device(k))
+
+    for k in range(1, INNER):
+        scatter(k).start()
+
+    gqs_copy.wait_recv()
     gm_far.wait_recv()
-    gqs_copy.wait_recv()
+
+    def rounded(value):
+        return value.astype(BF16).astype(F32)
 
     def back(t, carry):
+        upper, lower = carry
         conv = select(
-            jnp.dot(umat[t], gmx[pl.ds(0, 2 * K), lanes(t)], preferred_element_type=F32), K
+            jnp.dot(umat[t], gmx[t, pl.ds(0, 2 * K), :], preferred_element_type=F32), K
         )
         extra = select(
-            jnp.dot(xmat[t], gmx[pl.ds(K, 2 * K), lanes(t)], preferred_element_type=F32), 8
+            jnp.dot(xmat[t], gmx[t, pl.ds(K, 2 * K), :], preferred_element_type=F32), 8
         )
         skip = skip_ref[:, lanes(t)]
-        grad_gated = skip * gmx[pl.ds(0, K), lanes(t)].astype(F32) + conv
-        ek[t, pl.ds(0, length), :] = (grad_gated * sv[t, pl.ds(0, length), :]).astype(BF16).astype(F32)
-        ev[t, pl.ds(0, length), :] = (grad_gated * sk[t, pl.ds(0, length), :]).astype(BF16).astype(F32)
-        near = gmx[pl.ds(K, HEAD), lanes(t)].astype(F32)[:RIM]
+        grad_gated = skip * gmx[t, pl.ds(0, K), :].astype(F32) + conv
+        ek[t, pl.ds(0, length), :] = rounded(grad_gated * sv[t, pl.ds(0, length), :])
+        ev[t, pl.ds(0, length), :] = rounded(grad_gated * sk[t, pl.ds(0, length), :])
+        near = gmx[t, pl.ds(K, HEAD), :].astype(F32)[:RIM]
         grad_gated = skip * near + extra
-        ek[t, pl.ds(length, RIM), :] = (grad_gated * sv[t, pl.ds(length, RIM), :]).astype(BF16).astype(F32)
-        ev[t, pl.ds(length, RIM), :] = (grad_gated * sk[t, pl.ds(length, RIM), :]).astype(BF16).astype(F32)
+        ek[t, pl.ds(length, RIM), :] = rounded(grad_gated * sv[t, pl.ds(length, RIM), :])
+        ev[t, pl.ds(length, RIM), :] = rounded(grad_gated * sk[t, pl.ds(length, RIM), :])
         eq[t, pl.ds(length, RIM), :] = gqs_r[:, lanes(t)].astype(F32)
-        for s, (buf, values, out) in enumerate(((eq, xq, gq_out), (ek, xk, gk_out), (ev, xv, gv_out))):
+        blocks = []
+        for buf, values in ((eq, xq), (ek, xk), (ev, xv)):
             own = values[t, pl.ds(RIM, length), :]
-            result_sum = jnp.zeros((length, 128), F32)
             for j in range(KS):
                 moved = buf[t, pl.ds(j, length), :] * taps_m[j, pl.ds(RIM + j, length), :]
-                result_sum = result_sum + taps_w[t, pl.ds(s * 8 + j, 1), :] * moved
-                tsum[t, pl.ds(s * 8 + j, 1), :] = jnp.sum(moved * own, axis=0, keepdims=True)
-            out[:, lanes(t)] = result_sum.astype(BF16)
-        return carry
-
-    lax.fori_loop(0, tiles, back, 0)
-
-    short_sums = jnp.zeros((24, 128), F32)
-    for t in range(tiles):
-        spread = flag(iota((128, 128), 0) // GS + t * per == iota((128, 128), 1))
-        short_sums = short_sums + jnp.dot(
-            tsum[t], spread, precision=HIGH, preferred_element_type=F32
-        )
-    for s in range(3):
-        xs[10 + s] = short_sums[s * 8 : (s + 1) * 8]
-    for i in range(13, INNER):
-        xs[i] = jnp.zeros((8, 128), F32)
-
-    def scatter(k):
-        peer = inner_peer(k)
-        return pltpu.make_async_remote_copy(
-            src_ref=xs.at[peer],
-            dst_ref=first.at[lo],
-            send_sem=s1.at[k],
-            recv_sem=r1.at[lo],
-            device_id={"ctx": hi * INNER + peer},
-            device_id_type=MESH_ID,
-        )
-
-    def exchange(k):
-        return pltpu.make_async_remote_copy(
-            src_ref=second.at[hi],
-            dst_ref=second.at[hi],
-            send_sem=s2.at[k],
-            recv_sem=r2.at[hi],
-            device_id={"ctx": outer_peer(k) * INNER + lo},
-            device_id_type=MESH_ID,
-        )
-
-    def gather(k):
-        return pltpu.make_async_remote_copy(
-            src_ref=result.at[lo],
-            dst_ref=result.at[lo],
-            send_sem=s3.at[k],
-            recv_sem=r3.at[lo],
-            device_id={"ctx": hi * INNER + inner_peer(k)},
-            device_id_type=MESH_ID,
-        )
-
+                blocks.append(jnp.sum(moved * own, axis=0, keepdims=True))
+            blocks.append(jnp.zeros((1, 128), F32))
+        sums = jnp.concatenate(blocks, axis=0)
+        high = sums.astype(BF16)
+        rest_sums = sums - high.astype(F32)
+        middle = rest_sums.astype(BF16)
+        low = (rest_sums - middle.astype(F32)).astype(BF16)
+        channel = iota((128, 128), 0) // GS + t * per
+        spread = flag(channel == iota((128, 128), 1)).astype(BF16)
+        spread_high = flag(channel + 64 == iota((128, 128), 1)).astype(BF16)
+
+        def spread_sum(rows, onto):
+            parts = jnp.concatenate([high[rows], middle[rows], low[rows]], axis=0)
+            parts = jnp.dot(parts, onto, preferred_element_type=F32)
+            return parts[0:8] + parts[8:16] + parts[16:24]
+
+        upper = upper + spread_sum(slice(0, 8), spread) + spread_sum(slice(8, 16), spread_high)
+        lower = lower + spread_sum(slice(16, 24), spread)
+        return upper, lower
+
+    upper = jnp.zeros((8, 128), F32)
+    lower = jnp.zeros((8, 128), F32)
+    for c in range(CHUNKS):
+        gm_copies[c].wait_recv()
+        upper, lower = lax.fori_loop(c * each, (c + 1) * each, back, (upper, lower))
+        if c == CHUNKS // 2 - 1:
+            sums = xs[lo]
+            for k in range(1, INNER):
+                slot = inner_peer(INNER - k)
+                arrived(r1, first, slot)
+                sums = sums + first[slot]
+            second[hi] = sums
+            for k in range(1, outer):
+                exchange(k).start()
+    near_s[lo, pl.ds(0, 8), :] = upper
+    near_s[lo, pl.ds(8, 8), :] = lower
     for k in range(1, INNER):
-        scatter(k).start()
-    sums = xs[lo]
-    for k in range(1, INNER):
-        slot = inner_peer(INNER - k)
-        arrived(r1, first, slot)
-        sums = sums + first[slot]
-    second[hi] = sums
-    for k in range(1, outer):
-        exchange(k).start()
+        near_sums(k).start()
     for k in range(1, outer):
         arrived(r2, second, outer_peer(outer - k))
     sums = second[0]
@@ -510,35 +560,72 @@
     for k in range(1, INNER):
         gather(k).start()
 
-    for copy in (
-        tails,
-        tails2,
-        heads_k,
-        heads_v,
-        heads_back,
-        gated_copy,
-        gm_copy,
-        gm_far,
-        gqs_copy,
-    ):
+    def streams(t, carry):
+        for s, (buf, out) in enumerate(((eq, gq_b), (ek, gk_b), (ev, gv_b))):
+            result_sum = jnp.zeros((length, 128), F32)
+            for j in range(KS):
+                moved = buf[t, pl.ds(j, length), :] * taps_m[j, pl.ds(RIM + j, length), :]
+                result_sum = result_sum + taps_w[t, pl.ds(s * 8 + j, 1), :] * moved
+            out[:, lanes(t)] = result_sum.astype(BF16)
+        return carry
+
+    lax.fori_loop(0, tiles, streams, 0)
+    for store in stores[1:]:
+        store.start()
+
+    for k in range(1, INNER):
+        arrived(r4, near_s, inner_peer(INNER - k))
+    sums = near_s[0]
+    for i in range(1, INNER):
+        sums = sums + near_s[i]
+    far_s[hi] = sums
+    for k in range(1, outer):
+        far_sums(k).start()
+
+    for k in range(1, INNER):
+        arrived(r3, result, inner_peer(INNER - k))
+    for t in range(tiles):
+        glong_out[pl.ds(t * per, per), :] = result[t]
+    gskip_out[...] = result[8]
+    ggain_out[...] = result[9]
+    for copy in [tails, tails2, heads_k, heads_v, heads_back, gm_far, gqs_copy] + gated_copies + gm_copies:
         copy.wait_send()
     for k in range(1, tp_count):
         share(k).wait_send()
     for k in range(1, INNER):
         scatter(k).wait_send()
+        gather(k).wait_send()
+        near_sums(k).wait_send()
     for k in range(1, outer):
         exchange(k).wait_send()
-    for k in range(1, INNER):
-        arrived(r3, result, inner_peer(INNER - k))
-
-    for t in range(tiles):
-        glong_out[pl.ds(t * per, per), :] = result[t]
-    gskip_out[...] = result[8]
-    ggain_out[...] = result[9]
-    for s in range(3):
-        gshort_out[s] = result[10 + s].T[:groups, :KS]
-    for k in range(1, INNER):
-        gather(k).wait_send()
+
+    for k in range(1, outer):
+        arrived(r5, far_s, outer_peer(outer - k))
+    sums = far_s[0]
+    for i in range(1, outer):
+        sums = sums + far_s[i]
+    gshort_out[0] = sums[:KS, :groups]
+    gshort_out[1] = sums[:KS, 64 : 64 + groups]
+    gshort_out[2] = sums[8 : 8 + KS, :groups]
+    for k in range(1, outer):
+        far_sums(k).wait_send()
+    for store in stores:
+        store.wait()
+
+
+def finish(*refs):
+    half = (len(refs) - 2) // 3
+    came, left = refs[-2:]
+    bufs = refs[2 * half : 3 * half]
+    reads = [pltpu.make_async_copy(refs[i], bufs[i], came.at[i]) for i in range(half)]
+    writes = [pltpu.make_async_copy(bufs[i], refs[half + i], left.at[i]) for i in range(half)]
+    for copy in reads:
+        copy.start()
+    for read, write in zip(reads, writes):
+        read.wait()
+        write.start()
+    for copy in writes:
+        copy.wait()
 
 
 def shards(
@@ -565,13 +652,13 @@
             large,
             large,
             large,
-            jax.ShapeDtypeStruct((3, groups, KS), F32),
+            jax.ShapeDtypeStruct((3, KS, groups), F32),
             jax.ShapeDtypeStruct((groups, K), F32),
             jax.ShapeDtypeStruct((tiles, 128), F32),
             jax.ShapeDtypeStruct((tiles, 128), F32),
         ),
         in_specs=[pl.BlockSpec(memory_space=pltpu.SMEM)] + [vmem] * 9,
-        out_specs=(vmem,) * 8,
+        out_specs=(pl.BlockSpec(memory_space=pl.ANY),) * 4 + (vmem,) * 4,
         scratch_shapes=[
             pltpu.VMEM((3, RIM, width), BF16),
             pltpu.VMEM((3, RIM, width), BF16),
@@ -580,8 +667,8 @@
             pltpu.VMEM((HEAD, width), BF16),
             pltpu.VMEM((2, RIM, width), BF16),
             pltpu.VMEM((2, RIM, width), BF16),
-            pltpu.VMEM((2 * K, width), BF16),
-            pltpu.VMEM((3 * K, width), BF16),
+            pltpu.VMEM((tiles, 2 * K, 128), BF16),
+            pltpu.VMEM((tiles, 3 * K, 128), BF16),
             pltpu.VMEM((RIM, width), BF16),
             pltpu.VMEM((RIM, width), BF16),
             tiled(length + 2 * RIM),
@@ -608,14 +695,13 @@
             pltpu.VMEM((groups, K), F32),
             pltpu.VMEM((groups, K), F32),
             pltpu.VMEM((groups * 8, K), F32),
-            tiled(24),
             pltpu.VMEM((tp_count, 8, 128), F32),
             pltpu.VMEM((INNER, 8, 128), F32),
             pltpu.VMEM((INNER, 8, 128), F32),
             pltpu.VMEM((outer, 8, 128), F32),
             pltpu.VMEM((INNER, 8, 128), F32),
-            dma((9,)),
-            dma((9,)),
+            dma((7 + 2 * CHUNKS,)),
+            dma((7 + 2 * CHUNKS,)),
             dma((tp_count,)),
             dma((tp_count,)),
             dma((INNER,)),
@@ -624,6 +710,17 @@
             dma((outer,)),
             dma((INNER,)),
             dma((INNER,)),
+            pltpu.VMEM((INNER, 16, 128), F32),
+            pltpu.VMEM((outer, 16, 128), F32),
+            dma((INNER,)),
+            dma((INNER,)),
+            dma((outer,)),
+            dma((outer,)),
+            pltpu.VMEM((length, width), BF16),
+            pltpu.VMEM((length, width), BF16),
+            pltpu.VMEM((length, width), BF16),
+            pltpu.VMEM((length, width), BF16),
+            dma((4,)),
         ],
         compiler_params=pltpu.CompilerParams(collective_id=0, has_side_effects=True),
         name="operator",
@@ -634,12 +731,25 @@
         v_input,
         resid,
         cotangent,
-        short_filter,
+        jnp.transpose(short_filter, (0, 2, 1)),
         long_filter,
         skip.reshape(1, width),
         gain.reshape(1, width),
     )
-    return outs[:6] + (outs[6].reshape(width), outs[7].reshape(width))
+    outs = pl.pallas_call(
+        finish,
+        out_shape=tuple(jax.ShapeDtypeStruct(out.shape, out.dtype) for out in outs),
+        in_specs=[pl.BlockSpec(memory_space=pl.ANY)] * 8,
+        out_specs=(pl.BlockSpec(memory_space=pl.ANY),) * 8,
+        scratch_shapes=[pltpu.VMEM(out.shape, out.dtype) for out in outs] + [dma((8,)), dma((8,))],
+        name="finish",
+    )(*outs)
+    return outs[:4] + (
+        jnp.transpose(outs[4], (0, 2, 1)),
+        outs[5],
+        outs[6].reshape(width),
+        outs[7].reshape(width),
+    )
 
 
 def solution(mesh):

time: 77.2 us -> 62.7 us (0.81)
  the two profiles are of different devices: /device:TPU:6 before, /device:TPU:2 now
where the time goes in v1:
time: 62.7 us; the launch traced here: 62.6 us
  Pallas kernels  61.9 us (99%)
  between operations  0.64 us (1%)
    pallas_call x1, Pallas kernels, shards(): pl.pallas_call(functools.partial(body, count, tp_count), out_shape=(large...  59.9 us
    pallas_call x1, Pallas kernels, shards(): pl.pallas_call(finish, out_shape=tuple((jax.ShapeDtypeStruct(out.shape, o...  2.06 us

profile of v1, /device:TPU:2, one launch (start us, length us, event | category | flops | bytes accessed | tf_op | source)
XLA Modules:
  0.0 62.6 jit_solution(6707202013752341006)
XLA Ops:
  0.6 59.9 %operator.1 = (bf16[128,1024]{1,0:T(8,128)(2,1)}, bf16[128,1024]{1,0:T(8,128)(2,1)}, bf16[128,1024]{1,0:T(8,128)(2,1)}, bf16[128,1024]{1,0:T(8,128)(2,1)}, f32[3...) custom-call(s32[8]{0:T(128)} %lengths.1, bf16[128,1024]{1,0:T(8,128)(2,1)} %q_ref.1, ...), custom_call_target="tpu_custom_call" | custom-call | tf_op jit(solution)/shard_map/operator/pallas_call | solution.py:648
  60.5 2.1 %finish.1 = (bf16[128,1024]{1,0:T(8,128)(2,1)}, bf16[128,1024]{1,0:T(8,128)(2,1)}, bf16[128,1024]{1,0:T(8,128)(2,1)}, bf16[128,1024]{1,0:T(8,128)(2,1)}, f32[3,7...) custom-call(bf16[128,1024]{1,0:T(8,128)(2,1)} %get-tuple-element.24.refs_0_, ...), custom_call_target="tpu_custom_call" | custom-call | tf_op jit(solution)/shard_map/finish/pallas_call | solution.py:739

commit v2 on v1

--- a/solution.py
+++ b/solution.py
@@ -103,6 +103,7 @@
     r3,
     near_s,
     far_s,
+    tsum,
     s4,
     r4,
     s5,
@@ -255,9 +256,9 @@
     tails2.start()
     heads_k.start()
     heads_v.start()
-    heads_back.start()
     for copy in gated_copies:
         copy.start()
+    heads_back.start()
 
     def query_main(t, carry):
         xq[t, pl.ds(RIM, length), :] = q_ref[:, lanes(t)].astype(F32)
@@ -307,13 +308,11 @@
     tails2.wait_recv()
     heads_k.wait_recv()
     heads_v.wait_recv()
-    heads_back.wait_recv()
     for t in range(tiles):
         part = slice(t * 128, (t + 1) * 128)
         for s, buf in enumerate((xq, xk, xv)):
             buf[t, pl.ds(0, RIM), :] = tail_r[s, :, part].astype(F32)
         for s, (buf, prev, head) in enumerate(((xk, pk, headk_r), (xv, pv, headv_r))):
-            buf[t, pl.ds(RIM + length, RIM), :] = head_r[s, :, part].astype(F32)
             prev[t, pl.ds(0, RIM), :] = tail2_r[s, :, part].astype(F32)
             prev[t, pl.ds(RIM, HEAD), :] = head[:, part].astype(F32)
 
@@ -324,8 +323,6 @@
         sk[t, pl.ds(0, HEAD), :] = ks
         sv[t, pl.ds(0, HEAD), :] = vs
         gext[t, pl.ds(K, HEAD), :] = (ks * vs).astype(BF16)
-        sk[t, pl.ds(length, RIM), :] = short_sum(xk, t, 1, length, RIM, taps_m, RIM + length)
-        sv[t, pl.ds(length, RIM), :] = short_sum(xv, t, 2, length, RIM, taps_m, RIM + length)
         ks = short_sum(pk, t, 1, 0, HEAD, prev_m, 0)
         vs = short_sum(pv, t, 2, 0, HEAD, prev_m, 0)
         gext[t, pl.ds(0, HEAD), :] = (ks * vs).astype(BF16)
@@ -450,6 +447,7 @@
         xs[t] = turned[t * per : (t + 1) * per]
     for i in range(10, INNER):
         xs[i] = jnp.zeros((8, 128), F32)
+    tsum[...] = jnp.zeros_like(tsum)
 
     def copy_to(src, dst, send, recv, device):
         return pltpu.make_async_remote_copy(
@@ -485,6 +483,16 @@
     for k in range(1, INNER):
         scatter(k).start()
 
+    heads_back.wait_recv()
+
+    def gate_next(t, carry):
+        for s, buf in enumerate((xk, xv)):
+            buf[t, pl.ds(RIM + length, RIM), :] = head_r[s, :, lanes(t)].astype(F32)
+        sk[t, pl.ds(length, RIM), :] = short_sum(xk, t, 1, length, RIM, taps_m, RIM + length)
+        sv[t, pl.ds(length, RIM), :] = short_sum(xv, t, 2, length, RIM, taps_m, RIM + length)
+        return carry
+
+    lax.fori_loop(0, tiles, gate_next, 0)
     gqs_copy.wait_recv()
     gm_far.wait_recv()
 
@@ -492,7 +500,6 @@
         return value.astype(BF16).astype(F32)
 
     def back(t, carry):
-        upper, lower = carry
         conv = select(
             jnp.dot(umat[t], gmx[t, pl.ds(0, 2 * K), :], preferred_element_type=F32), K
         )
@@ -508,49 +515,51 @@
         ek[t, pl.ds(length, RIM), :] = rounded(grad_gated * sv[t, pl.ds(length, RIM), :])
         ev[t, pl.ds(length, RIM), :] = rounded(grad_gated * sk[t, pl.ds(length, RIM), :])
         eq[t, pl.ds(length, RIM), :] = gqs_r[:, lanes(t)].astype(F32)
-        blocks = []
-        for buf, values in ((eq, xq), (ek, xk), (ev, xv)):
+        for s, (buf, values) in enumerate(((eq, xq), (ek, xk), (ev, xv))):
             own = values[t, pl.ds(RIM, length), :]
             for j in range(KS):
                 moved = buf[t, pl.ds(j, length), :] * taps_m[j, pl.ds(RIM + j, length), :]
-                blocks.append(jnp.sum(moved * own, axis=0, keepdims=True))
-            blocks.append(jnp.zeros((1, 128), F32))
-        sums = jnp.concatenate(blocks, axis=0)
-        high = sums.astype(BF16)
-        rest_sums = sums - high.astype(F32)
-        middle = rest_sums.astype(BF16)
-        low = (rest_sums - middle.astype(F32)).astype(BF16)
-        channel = iota((128, 128), 0) // GS + t * per
-        spread = flag(channel == iota((128, 128), 1)).astype(BF16)
-        spread_high = flag(channel + 64 == iota((128, 128), 1)).astype(BF16)
-
-        def spread_sum(rows, onto):
-            parts = jnp.concatenate([high[rows], middle[rows], low[rows]], axis=0)
-            parts = jnp.dot(parts, onto, preferred_element_type=F32)
-            return parts[0:8] + parts[8:16] + parts[16:24]
-
-        upper = upper + spread_sum(slice(0, 8), spread) + spread_sum(slice(8, 16), spread_high)
-        lower = lower + spread_sum(slice(16, 24), spread)
-        return upper, lower
-
-    upper = jnp.zeros((8, 128), F32)
-    lower = jnp.zeros((8, 128), F32)
+                tsum[t, pl.ds(s * 8 + j, 1), :] = jnp.sum(moved * own, axis=0, keepdims=True)
+        return carry
+
     for c in range(CHUNKS):
         gm_copies[c].wait_recv()
-        upper, lower = lax.fori_loop(c * each, (c + 1) * each, back, (upper, lower))
-        if c == CHUNKS // 2 - 1:
-            sums = xs[lo]
-            for k in range(1, INNER):
-                slot = inner_peer(INNER - k)
-                arrived(r1, first, slot)
-                sums = sums + first[slot]
-            second[hi] = sums
-            for k in range(1, outer):
-                exchange(k).start()
-    near_s[lo, pl.ds(0, 8), :] = upper
-    near_s[lo, pl.ds(8, 8), :] = lower
+        lax.fori_loop(c * each, (c + 1) * each, back, 0)
+    spread_sums = jnp.zeros((72, 128), F32)
+    for t in range(tiles):
+        sums = tsum[t]
+        high = sums.astype(BF16).astype(F32)
+        middle = (sums - high).astype(BF16).astype(F32)
+        parts = jnp.concatenate([high, middle, sums - high - middle], axis=0).astype(BF16)
+        spread = flag(row // GS + t * per == col).astype(BF16)
+        spread_sums = spread_sums + jnp.dot(parts, spread, preferred_element_type=F32)
+    spread_sums = spread_sums[0:24] + spread_sums[24:48] + spread_sums[48:72]
+    near_s[lo, pl.ds(0, 8), :] = spread_sums[0:8] + pltpu.roll(spread_sums[8:16], 64, 1)
+    near_s[lo, pl.ds(8, 8), :] = spread_sums[16:24]
     for k in range(1, INNER):
         near_sums(k).start()
+    sums = xs[lo]
+    for k in range(1, INNER):
+        slot = inner_peer(INNER - k)
+        arrived(r1, first, slot)
+        sums = sums + first[slot]
+    second[hi] = sums
+    for k in range(1, outer):
+        exchange(k).start()
+
+    def streams(t, carry):
+        for s, (buf, out) in enumerate(((eq, gq_b), (ek, gk_b), (ev, gv_b))):
+            result_sum = jnp.zeros((length, 128), F32)
+            for j in range(KS):
+                moved = buf[t, pl.ds(j, length), :] * taps_m[j, pl.ds(RIM + j, length), :]
+                result_sum = result_sum + taps_w[t, pl.ds(s * 8 + j, 1), :] * moved
+            out[:, lanes(t)] = result_sum.astype(BF16)
+        return carry
+
+    lax.fori_loop(0, tiles, streams, 0)
+    for store in stores[1:]:
+        store.start()
+
     for k in range(1, outer):
         arrived(r2, second, outer_peer(outer - k))
     sums = second[0]
@@ -559,19 +568,6 @@
     result[lo] = sums
     for k in range(1, INNER):
         gather(k).start()
-
-    def streams(t, carry):
-        for s, (buf, out) in enumerate(((eq, gq_b), (ek, gk_b), (ev, gv_b))):
-            result_sum = jnp.zeros((length, 128), F32)
-            for j in range(KS):
-                moved = buf[t, pl.ds(j, length), :] * taps_m[j, pl.ds(RIM + j, length), :]
-                result_sum = result_sum + taps_w[t, pl.ds(s * 8 + j, 1), :] * moved
-            out[:, lanes(t)] = result_sum.astype(BF16)
-        return carry
-
-    lax.fori_loop(0, tiles, streams, 0)
-    for store in stores[1:]:
-        store.start()
 
     for k in range(1, INNER):
         arrived(r4, near_s, inner_peer(INNER - k))
@@ -712,6 +708,7 @@
             dma((INNER,)),
             pltpu.VMEM((INNER, 16, 128), F32),
             pltpu.VMEM((outer, 16, 128), F32),
+            tiled(24),
             dma((INNER,)),
             dma((INNER,)),
             dma((outer,)),

time: 62.7 us -> 61 us (0.973)
  Pallas kernels: 61.9 us -> 60.2 us
    pallas_call x1, Pallas kernels: 59.9 us -> 58.1 us  [shards(): pl.pallas_call(functools.partial(body, count, tp_count), out_shape=(large...]
where the time goes in v2:
time: 61 us; the launch traced here: 60.8 us
  Pallas kernels  60.2 us (99%)
  between operations  0.64 us (1%)
    pallas_call x1, Pallas kernels, shards(): pl.pallas_call(functools.partial(body, count, tp_count), out_shape=(large...  58.1 us
    pallas_call x1, Pallas kernels, shards(): pl.pallas_call(finish, out_shape=tuple((jax.ShapeDtypeStruct(out.shape, o...  2.06 us

profile of v2, /device:TPU:2, one launch (start us, length us, event | category | flops | bytes accessed | tf_op | source)
XLA Modules:
  0.0 60.8 jit_solution(10565710694435181888)
XLA Ops:
  0.6 58.1 %operator.1 = (bf16[128,1024]{1,0:T(8,128)(2,1)}, bf16[128,1024]{1,0:T(8,128)(2,1)}, bf16[128,1024]{1,0:T(8,128)(2,1)}, bf16[128,1024]{1,0:T(8,128)(2,1)}, f32[3...) custom-call(s32[8]{0:T(128)} %lengths.1, bf16[128,1024]{1,0:T(8,128)(2,1)} %q_ref.1, ...), custom_call_target="tpu_custom_call" | custom-call | tf_op jit(solution)/shard_map/operator/pallas_call | solution.py:644
  58.7 2.1 %finish.1 = (bf16[128,1024]{1,0:T(8,128)(2,1)}, bf16[128,1024]{1,0:T(8,128)(2,1)}, bf16[128,1024]{1,0:T(8,128)(2,1)}, bf16[128,1024]{1,0:T(8,128)(2,1)}, f32[3,7...) custom-call(bf16[128,1024]{1,0:T(8,128)(2,1)} %get-tuple-element.24.refs_0_, ...), custom_call_target="tpu_custom_call" | custom-call | tf_op jit(solution)/shard_map/finish/pallas_call | solution.py:736

commit v3 on v2

--- a/solution.py
+++ b/solution.py
@@ -37,8 +37,8 @@
     q_ref,
     k_ref,
     v_ref,
-    resid_ref,
-    cot_ref,
+    resid_hbm,
+    cot_hbm,
     short_ref,
     long_ref,
     skip_ref,
@@ -108,11 +108,9 @@
     r4,
     s5,
     r5,
-    normed_b,
-    gq_b,
-    gk_b,
-    gv_b,
-    os,
+    resid_ref,
+    cot_ref,
+    ls,
 ):
     length, width = q_ref.shape
     tiles = width // 128
@@ -191,6 +189,13 @@
     head_s[0] = k_ref[0:HEAD, :].astype(F32)[:RIM].astype(BF16)
     head_s[1] = v_ref[0:HEAD, :].astype(F32)[:RIM].astype(BF16)
 
+    loads = [
+        pltpu.make_async_copy(resid_hbm, resid_ref, ls.at[0]),
+        pltpu.make_async_copy(cot_hbm, cot_ref, ls.at[1]),
+    ]
+    for load in loads:
+        load.start()
+
     starts = []
     at = jnp.int32(0)
     for i in range(lengths.shape[0]):
@@ -210,6 +215,53 @@
     pos = position(token)
     for j in range(KS):
         taps_m[j] = flag((pos >= j) & (token < total))
+    picks = flag(iota((groups, width), 1) // GS == iota((groups, width), 0)).astype(BF16)
+    for s in range(3):
+        table = jnp.dot(short_ref[s], picks, preferred_element_type=F32)
+        for t in range(tiles):
+            taps_w[t, pl.ds(s * 8, KS), :] = table[:, t * 128 : (t + 1) * 128]
+
+    def lanes(t):
+        return pl.ds(pl.multiple_of(t * 128, 128), 128)
+
+    def short_sum(buf, t, s, first_row, rows, mask, mask_row):
+        result_sum = taps_w[t, pl.ds(s * 8, 1), :] * buf[t, pl.ds(RIM + first_row, rows), :]
+        for j in range(1, KS):
+            moved = buf[t, pl.ds(RIM + first_row - j, rows), :]
+            result_sum = result_sum + taps_w[t, pl.ds(s * 8 + j, 1), :] * (
+                moved * mask[j, pl.ds(mask_row, rows), :]
+            )
+        return result_sum
+
+    rest = length - HEAD
+
+    def gate_main(t, carry):
+        xk[t, pl.ds(RIM, length), :] = k_ref[:, lanes(t)].astype(F32)
+        xv[t, pl.ds(RIM, length), :] = v_ref[:, lanes(t)].astype(F32)
+        ks = short_sum(xk, t, 1, HEAD, rest, taps_m, RIM + HEAD)
+        vs = short_sum(xv, t, 2, HEAD, rest, taps_m, RIM + HEAD)
+        sk[t, pl.ds(HEAD, rest), :] = ks
+        sv[t, pl.ds(HEAD, rest), :] = vs
+        gext[t, pl.ds(K + HEAD, rest), :] = (ks * vs).astype(BF16)
+        return carry
+
+    lax.fori_loop(0, tiles, gate_main, 0)
+    pl.semaphore_wait(barrier, 4 + tp_count - 1 + INNER - 1 + outer - 1)
+    tails.start()
+    tails2.start()
+    heads_k.start()
+    heads_v.start()
+    for copy in gated_copies:
+        copy.start()
+    heads_back.start()
+
+    def query_main(t, carry):
+        xq[t, pl.ds(RIM, length), :] = q_ref[:, lanes(t)].astype(F32)
+        sq[t, pl.ds(HEAD, rest), :] = short_sum(xq, t, 0, HEAD, rest, taps_m, RIM + HEAD)
+        return carry
+
+    lax.fori_loop(0, tiles, query_main, 0)
+
     token = base - K + iota((HEAD, 128), 0)
     pos = position(token)
     for j in range(KS):
@@ -219,54 +271,6 @@
     pos = position(base + row)
     mats[0] = flag((col > row) & (pos >= row - col + K))
     mats[1] = flag((col <= row) & (pos >= row - col))
-
-    picks = flag(iota((groups, width), 1) // GS == iota((groups, width), 0)).astype(BF16)
-    for s in range(3):
-        table = jnp.dot(short_ref[s], picks, preferred_element_type=F32)
-        for t in range(tiles):
-            taps_w[t, pl.ds(s * 8, KS), :] = table[:, t * 128 : (t + 1) * 128]
-
-    def lanes(t):
-        return pl.ds(pl.multiple_of(t * 128, 128), 128)
-
-    def short_sum(buf, t, s, first_row, rows, mask, mask_row):
-        result_sum = taps_w[t, pl.ds(s * 8, 1), :] * buf[t, pl.ds(RIM + first_row, rows), :]
-        for j in range(1, KS):
-            moved = buf[t, pl.ds(RIM + first_row - j, rows), :]
-            result_sum = result_sum + taps_w[t, pl.ds(s * 8 + j, 1), :] * (
-                moved * mask[j, pl.ds(mask_row, rows), :]
-            )
-        return result_sum
-
-    rest = length - HEAD
-
-    def gate_main(t, carry):
-        xk[t, pl.ds(RIM, length), :] = k_ref[:, lanes(t)].astype(F32)
-        xv[t, pl.ds(RIM, length), :] = v_ref[:, lanes(t)].astype(F32)
-        ks = short_sum(xk, t, 1, HEAD, rest, taps_m, RIM + HEAD)
-        vs = short_sum(xv, t, 2, HEAD, rest, taps_m, RIM + HEAD)
-        sk[t, pl.ds(HEAD, rest), :] = ks
-        sv[t, pl.ds(HEAD, rest), :] = vs
-        gext[t, pl.ds(K + HEAD, rest), :] = (ks * vs).astype(BF16)
-        return carry
-
-    lax.fori_loop(0, tiles, gate_main, 0)
-    pl.semaphore_wait(barrier, 4 + tp_count - 1 + INNER - 1 + outer - 1)
-    tails.start()
-    tails2.start()
-    heads_k.start()
-    heads_v.start()
-    for copy in gated_copies:
-        copy.start()
-    heads_back.start()
-
-    def query_main(t, carry):
-        xq[t, pl.ds(RIM, length), :] = q_ref[:, lanes(t)].astype(F32)
-        sq[t, pl.ds(HEAD, rest), :] = short_sum(xq, t, 0, HEAD, rest, taps_m, RIM + HEAD)
-        return carry
-
-    lax.fori_loop(0, tiles, query_main, 0)
-
     pos = position(base + col)
     mats[2] = flag((col >= row) & (pos >= col - row))
     token = base + K + col
@@ -350,6 +354,8 @@
         products = products + gain_ref[:, lanes(t)] * cot_ref[:, lanes(t)].astype(F32) * summed
         return squares, products
 
+    for load in loads:
+        load.wait()
     zero = jnp.zeros((length, 128), F32)
     squares, products = zero, zero
     for c in range(CHUNKS):
@@ -394,7 +400,7 @@
         summed = summed_s[t]
         gain = gain_ref[:, lanes(t)]
         cot = cot_ref[:, lanes(t)].astype(F32)
-        normed_b[:, lanes(t)] = (gain * summed * inverse).astype(BF16)
+        normed_out[:, lanes(t)] = (gain * summed * inverse).astype(BF16)
         grad_sum = inverse * (gain * cot - summed * mats[5])
         grad_mixed = (grad_sum * sq[t]).astype(BF16)
         gmx[t, pl.ds(0, K), :] = grad_mixed
@@ -411,13 +417,6 @@
     gm_far.start()
     for copy in gm_copies:
         copy.start()
-    stores = [
-        pltpu.make_async_copy(buf, out, os.at[i])
-        for i, (buf, out) in enumerate(
-            ((normed_b, normed_out), (gq_b, gq_out), (gk_b, gk_out), (gv_b, gv_out))
-        )
-    ]
-    stores[0].start()
 
     def correlate(t, carry):
         grad_mixed = gmx[t, pl.ds(0, K), :]
@@ -548,7 +547,7 @@
         exchange(k).start()
 
     def streams(t, carry):
-        for s, (buf, out) in enumerate(((eq, gq_b), (ek, gk_b), (ev, gv_b))):
+        for s, (buf, out) in enumerate(((eq, gq_out), (ek, gk_out), (ev, gv_out))):
             result_sum = jnp.zeros((length, 128), F32)
             for j in range(KS):
                 moved = buf[t, pl.ds(j, length), :] * taps_m[j, pl.ds(RIM + j, length), :]
@@ -557,8 +556,6 @@
         return carry
 
     lax.fori_loop(0, tiles, streams, 0)
-    for store in stores[1:]:
-        store.start()
 
     for k in range(1, outer):
         arrived(r2, second, outer_peer(outer - k))
@@ -605,22 +602,15 @@
     gshort_out[2] = sums[8 : 8 + KS, :groups]
     for k in range(1, outer):
         far_sums(k).wait_send()
-    for store in stores:
-        store.wait()
 
 
 def finish(*refs):
-    half = (len(refs) - 2) // 3
-    came, left = refs[-2:]
-    bufs = refs[2 * half : 3 * half]
-    reads = [pltpu.make_async_copy(refs[i], bufs[i], came.at[i]) for i in range(half)]
-    writes = [pltpu.make_async_copy(bufs[i], refs[half + i], left.at[i]) for i in range(half)]
-    for copy in reads:
+    half = (len(refs) - 1) // 2
+    left = refs[-1]
+    copies = [pltpu.make_async_copy(refs[i], refs[half + i], left.at[i]) for i in range(half)]
+    for copy in copies:
         copy.start()
-    for read, write in zip(reads, writes):
-        read.wait()
-        write.start()
-    for copy in writes:
+    for copy in copies:
         copy.wait()
 
 
@@ -635,7 +625,7 @@
     tp_count = lax.axis_size("tp")
     outer = count // INNER
     vmem = pl.BlockSpec(memory_space=pltpu.VMEM)
-    large = jax.ShapeDtypeStruct((length, width), BF16)
+    large = pltpu.VMEM((length, width), BF16)
 
     def tiled(rows):
         return pltpu.VMEM((tiles, rows, 128), F32)
@@ -648,13 +638,13 @@
             large,
             large,
             large,
-            jax.ShapeDtypeStruct((3, KS, groups), F32),
-            jax.ShapeDtypeStruct((groups, K), F32),
-            jax.ShapeDtypeStruct((tiles, 128), F32),
-            jax.ShapeDtypeStruct((tiles, 128), F32),
+            pltpu.VMEM((3, KS, groups), F32),
+            pltpu.VMEM((groups, K), F32),
+            pltpu.VMEM((tiles, 128), F32),
+            pltpu.VMEM((tiles, 128), F32),
         ),
-        in_specs=[pl.BlockSpec(memory_space=pltpu.SMEM)] + [vmem] * 9,
-        out_specs=(pl.BlockSpec(memory_space=pl.ANY),) * 4 + (vmem,) * 4,
+        in_specs=[pl.BlockSpec(memory_space=pltpu.SMEM)] + [vmem] * 3 + [pl.BlockSpec(memory_space=pl.ANY)] * 2 + [vmem] * 4,
+        out_specs=(vmem,) * 8,
         scratch_shapes=[
             pltpu.VMEM((3, RIM, width), BF16),
             pltpu.VMEM((3, RIM, width), BF16),
@@ -715,9 +705,7 @@
             dma((outer,)),
             pltpu.VMEM((length, width), BF16),
             pltpu.VMEM((length, width), BF16),
-            pltpu.VMEM((length, width), BF16),
-            pltpu.VMEM((length, width), BF16),
-            dma((4,)),
+            dma((2,)),
         ],
         compiler_params=pltpu.CompilerParams(collective_id=0, has_side_effects=True),
         name="operator",
@@ -736,11 +724,11 @@
     outs = pl.pallas_call(
         finish,
         out_shape=tuple(jax.ShapeDtypeStruct(out.shape, out.dtype) for out in outs),
-        in_specs=[pl.BlockSpec(memory_space=pl.ANY)] * 8,
+        in_specs=[vmem] * 8,
         out_specs=(pl.BlockSpec(memory_space=pl.ANY),) * 8,
-        scratch_shapes=[pltpu.VMEM(out.shape, out.dtype) for out in outs] + [dma((8,)), dma((8,))],
+        scratch_shapes=[dma((8,))],
         name="finish",
-    )(*outs)
+    )(*[pltpu.with_memory_space_constraint(out, pltpu.VMEM) for out in outs])
     return outs[:4] + (
         jnp.transpose(outs[4], (0, 2, 1)),
         outs[5],

time: 61 us -> 59.1 us (0.969)
  Pallas kernels: 60.2 us -> 58.3 us
    pallas_call x1, Pallas kernels: 2.06 us -> 1.04 us  [shards(): pl.pallas_call(finish, out_shape=tuple((jax.ShapeDtypeStruct(out.shape, o...]
    pallas_call x1, Pallas kernels: 58.1 us -> 57.3 us  [shards(): pl.pallas_call(functools.partial(body, count, tp_count), out_shape=(large...]
where the time goes in v3:
time: 59.1 us; the launch traced here: 59 us
  Pallas kernels  58.3 us (99%)
  between operations  0.64 us (1%)
    pallas_call x1, Pallas kernels, shards(): pl.pallas_call(functools.partial(body, count, tp_count), out_shape=(large...  57.3 us

profile of v3, /device:TPU:2, one launch (start us, length us, event | category | flops | bytes accessed | tf_op | source)
XLA Modules:
  0.0 59.0 jit_solution(1035050489366170256)
XLA Ops:
  0.6 57.3 %operator.1 = (bf16[128,1024]{1,0:T(8,128)(2,1)S(1)}, bf16[128,1024]{1,0:T(8,128)(2,1)S(1)}, bf16[128,1024]{1,0:T(8,128)(2,1)S(1)}, bf16[128,1024]{1,0:T(8,128)(...) custom-call(s32[8]{0:T(128)} %lengths.1, ...), custom_call_target="tpu_custom_call" | custom-call | tf_op jit(solution)/shard_map/operator/pallas_call | solution.py:634
  57.9 1.0 %finish.1 = (bf16[128,1024]{1,0:T(8,128)(2,1)}, bf16[128,1024]{1,0:T(8,128)(2,1)}, bf16[128,1024]{1,0:T(8,128)(2,1)}, bf16[128,1024]{1,0:T(8,128)(2,1)}, f32[3,7...) custom-call(bf16[128,1024]{1,0:T(8,128)(2,1)S(1)} %get-tuple-element.24.refs_0_, ...), custom_call_target="tpu_custom_call" | custom-call | tf_op jit(solution)/shard_map/finish/pallas_call | solution.py:724

commit v4 on v3

--- a/solution.py
+++ b/solution.py
@@ -20,6 +20,10 @@
 RIM = 8
 HEAD = 16
 CHUNKS = 4
+
+
+def far_first(ring):
+    return sorted(range(1, ring), key=lambda k: -min(k, ring - k))
 
 
 def iota(shape, axis):
@@ -479,7 +483,7 @@
     def far_sums(k):
         return copy_to(far_s.at[hi], far_s.at[hi], s5.at[k], r5.at[hi], outer_device(k))
 
-    for k in range(1, INNER):
+    for k in far_first(INNER):
         scatter(k).start()
 
     heads_back.wait_recv()
@@ -535,7 +539,7 @@
     spread_sums = spread_sums[0:24] + spread_sums[24:48] + spread_sums[48:72]
     near_s[lo, pl.ds(0, 8), :] = spread_sums[0:8] + pltpu.roll(spread_sums[8:16], 64, 1)
     near_s[lo, pl.ds(8, 8), :] = spread_sums[16:24]
-    for k in range(1, INNER):
+    for k in far_first(INNER):
         near_sums(k).start()
     sums = xs[lo]
     for k in range(1, INNER):
@@ -543,7 +547,7 @@
         arrived(r1, first, slot)
         sums = sums + first[slot]
     second[hi] = sums
-    for k in range(1, outer):
+    for k in far_first(outer):
         exchange(k).start()
 
     def streams(t, carry):
@@ -563,7 +567,7 @@
     for i in range(1, outer):
         sums = sums + second[i]
     result[lo] = sums
-    for k in range(1, INNER):
+    for k in far_first(INNER):
         gather(k).start()
 
     for k in range(1, INNER):
@@ -572,7 +576,7 @@
     for i in range(1, INNER):
         sums = sums + near_s[i]
     far_s[hi] = sums
-    for k in range(1, outer):
+    for k in far_first(outer):
         far_sums(k).start()
 
     for k in range(1, INNER):

time: 59.1 us -> 59 us (level)
  no operation moved by 1% of the time
where the time goes in v4:
time: 59 us; the launch traced here: 58.9 us
  Pallas kernels  58.2 us (99%)
  between operations  0.64 us (1%)
    pallas_call x1, Pallas kernels, shards(): pl.pallas_call(functools.partial(body, count, tp_count), out_shape=(large...  57.2 us

profile of v4, /device:TPU:2, one launch (start us, length us, event | category | flops | bytes accessed | tf_op | source)
XLA Modules:
  0.0 58.9 jit_solution(8940045824783880519)
XLA Ops:
  0.6 57.2 %operator.1 = (bf16[128,1024]{1,0:T(8,128)(2,1)S(1)}, bf16[128,1024]{1,0:T(8,128)(2,1)S(1)}, bf16[128,1024]{1,0:T(8,128)(2,1)S(1)}, bf16[128,1024]{1,0:T(8,128)(...) custom-call(s32[8]{0:T(128)} %lengths.1, ...), custom_call_target="tpu_custom_call" | custom-call | tf_op jit(solution)/shard_map/operator/pallas_call | solution.py:638
  57.8 1.0 %finish.1 = (bf16[128,1024]{1,0:T(8,128)(2,1)}, bf16[128,1024]{1,0:T(8,128)(2,1)}, bf16[128,1024]{1,0:T(8,128)(2,1)}, bf16[128,1024]{1,0:T(8,128)(2,1)}, f32[3,7...) custom-call(bf16[128,1024]{1,0:T(8,128)(2,1)S(1)} %get-tuple-element.24.refs_0_, ...), custom_call_target="tpu_custom_call" | custom-call | tf_op jit(solution)/shard_map/finish/pallas_call | solution.py:728
